TPU v7x, 32 devices: a whole 2x2x4 slice. The times are simulated.
32 devices in a mesh: rows: 8 (over y, x, core), rhs: 4 (over z).
Axes of the slice: x: 2, y: 2, z: 4, core: 2. Of those that a mesh axis runs over, the one named last changes fastest.
Arguments:
- samples: float32 [65536, 16], P(('rows', 'rhs')), may hold values from -5 to 5
- freq_table: float32 [4096, 16], replicated, may hold values from -3 to 3
- feature_seeds: int32 [512], replicated, may hold values from 0 to 4095
- phases: float32 [512], replicated, may hold values from -3.140625 to 3.140625
- treatment_features: bfloat16 [65536, 512], P('rows', 'rhs'), may hold values from -2.5 to 2.5, as said below
Outputs:
- coefficients: float32 [512, 512], replicated
- fitted: float32 [65536, 512], P(('rows', 'rhs'))
Inputs may be any that keep to these rules, and one draw needn't show every extreme that they name: `treatment_features`: treatment features depend on the instrument values.
All inputs are finite; a program needn't handle non-finite values.
Results may differ from a plain program's by a relative error of at most 0.0008.
The roundings to bfloat16 on the way count: a program that leaves them out, or rounds other values in their place, can miss the bound.
Values may be sent and summed in bfloat16 or wider, within the bound.
A program may use at most 64 MiB of HBM per device.

v0:
```python
import jax
import jax.numpy as jnp
from jax import lax
from jax.sharding import PartitionSpec as P

ridge = 0.05


def solve_with(factor, right):
    lower = lax.linalg.triangular_solve(factor, right, left_side=True, lower=True)
    return lax.linalg.triangular_solve(factor, lower, left_side=True, lower=True, transpose_a=True)


def features_of(values, freqs, phases):
    angles = (
        jnp.dot(
            values, freqs.T, precision=lax.Precision.HIGHEST, preferred_element_type=jnp.float32
        )
        + phases
    )
    return (jnp.sqrt(jnp.float32(2.0)) * jnp.cos(angles)).astype(jnp.bfloat16)


def body(samples, freq_table, feature_seeds, phases, treatment_features):
    own_rows = samples.shape[0]
    count = own_rows * lax.axis_size("rows") * lax.axis_size("rhs")
    freqs = freq_table[feature_seeds]
    contract = (((0,), (0,)), ((), ()))
    instruments = features_of(samples, freqs, phases)
    gram_part = lax.dot_general(
        instruments, instruments, contract, preferred_element_type=jnp.float32
    )
    gram = lax.psum(gram_part, ("rows", "rhs")) / count
    gram = gram + ridge * jnp.eye(gram.shape[0], dtype=jnp.float32)
    factor = jnp.linalg.cholesky(gram)
    targets = lax.all_to_all(treatment_features, "rhs", split_axis=0, concat_axis=1, tiled=True)
    cross_part = lax.dot_general(instruments, targets, contract, preferred_element_type=jnp.float32)
    cross = lax.psum(cross_part, ("rows", "rhs")) / count
    coefficients = solve_with(factor, cross)
    fitted = jnp.dot(
        instruments, coefficients.astype(jnp.bfloat16), preferred_element_type=jnp.float32
    )
    return (coefficients, fitted)


def solution(mesh):
    placed = (P(("rows", "rhs"), None), P(), P(), P(), P("rows", "rhs"))
    return jax.shard_map(
        body, mesh=mesh, in_specs=placed, out_specs=(P(), P(("rows", "rhs"), None)), check_vma=False
    )
```

profile of v0, /device:TPU:0, one launch (start us, length us, event | category | flops | bytes accessed | tf_op | source)
XLA Modules:
  0.0 364.8 jit_solution(18324534306063840201)
XLA Ops:
  7.2 6.5 %all-to-all-start = ((bf16[4,2048,128]{2,1,0:T(8,128)(2,1)}), bf16[4,2048,128]{2,1,0:T(8,128)(2,1)S(1)}, u32[]{:S(2)}, u32[]{:S(2)}) async-start(bf16[4,2048,128]{2,1,0:T(8,128)(2,1)} %bitcast.66), calls=%async_computation | async-start | bytes 4194304 | tf_op jit(solution)/shard_map/all_to_all | solution.py:36
  13.7 1.9 copy.31
  15.7 2.6 gather_fusion
  18.3 17.9 %multiply_convert_fusion = bf16[512,2048]{1,0:T(8,128)(2,1)S(1)} fusion(f32[512,16]{1,0:T(8,128)S(1)} %gather_fusion, f32[2048,16]{0,1:T(8,128)S(1)} %copy-done, f32[512]{0:T(512)S(1)} %copy-done.8), kind=kOutput, calls=%fused_computation.3 | convolution fusion | flops 204472320 | bytes 2263040 | tf_op jit(solution)/shard_map/dot_general | solution.py:16
  36.3 1.3 copy-done.3
  37.6 2.3 fusion.50
  39.8 22.0 %all-to-all-done = bf16[4,2048,128]{2,1,0:T(8,128)(2,1)S(1)} async-done(((bf16[4,2048,128]{2,1,0:T(8,128)(2,1)}), bf16[4,2048,128]{2,1,0:T(8,128)(2,1)S(1)}, u32[]{:S(2)}, u32[]{:S(2)}) %all-to-all-start) | async-done | bytes 2097184 | tf_op jit(solution)/shard_map/all_to_all | solution.py:36
  61.9 3.1 copy.42
  65.0 4.5 %fusion.51 = f32[512,512]{0,1:T(8,128)} fusion(bf16[512,2048]{1,0:T(8,128)(2,1)} %copy-done.3, bf16[2048,512]{0,1:T(8,128)(2,1)} %bitcast.67), kind=kOutput, calls=%fused_computation.97 | convolution fusion | flops 1073741824 | bytes 5242880 | tf_op jit(solution)/shard_map/dot_general | solution.py:37
  69.5 133.9 %all-reduce.4.cloned.1.call-done = (f32[512,512]{0,1:T(8,128)}, f32[512,512]{0,1:T(8,128)}) async-done(((f32[512,512]{0,1:T(8,128)}, f32[512,512]{0,1:T(8,128)}), (f32[512,512]{0,1:T(8,128)}, f32[512,512]{0,1:T(8,128)})) %all-reduce.4.cloned.1.call-update) | async-done | bytes 2097168 | tf_op jit(solution)/shard_map/psum | solution.py:38
  203.4 2.8 select_add_fusion
  206.2 1.6 copy.33
  209.1 11.7 %cholesky.103 = f32[128,128]{1,0:T(8,128)S(1)} custom-call(f32[128,128]{1,0:T(8,128)S(1)} %cholesky.263), custom_call_target="Cholesky" | custom-call | tf_op jit(solution)/shard_map/jit(cholesky)/cholesky | solution.py:35
  220.9 9.8 %custom-call.32 = f32[1,128,128]{1,2,0:T(8,128)S(1)} custom-call(f32[1,128,128]{2,1,0:T(8,128)S(1)} %get-tuple-element.39), custom_call_target="InvertDiagBlocksLowerTriangular" | custom-call | tf_op jit(solution)/shard_map/jit(cholesky)/cholesky | solution.py:35
  230.7 1.2 fusion.25
  232.0 1.3 convolution_subtract_fusion.6
  233.4 11.9 %cholesky.215 = f32[128,128]{1,0:T(8,128)S(1)} custom-call(f32[128,128]{1,0:T(8,128)S(1)} %cholesky.267), custom_call_target="Cholesky" | custom-call | tf_op jit(solution)/shard_map/jit(cholesky)/cholesky | solution.py:35
  245.4 9.8 %custom-call.33 = f32[1,128,128]{1,2,0:T(8,128)S(1)} custom-call(f32[1,128,128]{2,1,0:T(8,128)S(1)} %get-tuple-element.37), custom_call_target="InvertDiagBlocksLowerTriangular" | custom-call | tf_op jit(solution)/shard_map/jit(cholesky)/cholesky | solution.py:35
  255.7 1.5 convolution_subtract_fusion.7
  257.2 11.7 %cholesky.236 = f32[128,128]{1,0:T(8,128)S(1)} custom-call(f32[128,128]{1,0:T(8,128)S(1)} %cholesky.272), custom_call_target="Cholesky" | custom-call | tf_op jit(solution)/shard_map/jit(cholesky)/cholesky | solution.py:35
  269.1 9.8 %custom-call.34 = f32[1,128,128]{1,2,0:T(8,128)S(1)} custom-call(f32[1,128,128]{2,1,0:T(8,128)S(1)} %get-tuple-element.35), custom_call_target="InvertDiagBlocksLowerTriangular" | custom-call | tf_op jit(solution)/shard_map/jit(cholesky)/cholesky | solution.py:35
  279.2 1.3 convolution_subtract_fusion.8
  280.5 11.9 %cholesky.253 = f32[128,128]{1,0:T(8,128)S(1)} custom-call(f32[128,128]{1,0:T(8,128)S(1)} %convolution_subtract_fusion.8), custom_call_target="Cholesky" | custom-call | tf_op jit(solution)/shard_map/jit(cholesky)/cholesky | solution.py:35
  297.9 8.9 %while.1 = (s32[]{:T(128)}, f32[512,512]{0,1:T(8,128)S(1)}, s32[4,2]{0,1:T(2,128)S(1)}, f32[4,128,128]{2,1,0:T(8,128)S(1)}, s32[]{:T(128)}) while((s32[]{:T(128)}, f32[512,512]{0,1:T(8,128)S(1)}, s32[4,2]{0,1:T(2,128)S(1)}, f32[4,128,128]{2,1,0:T(8,128)S(1)}, s32[]{:T(128)}) %tuple.30), condition=%wide.while_cond, body=%wide.while_body.sunk | while | flops 2 | bytes 393329 | solution.py:11
  298.6 1.4 dynamic-slice.7
  300.8 1.4 dynamic-slice.7
  303.0 1.4 dynamic-slice.7
  305.3 1.4 dynamic-slice.7
  306.8 39.3 %custom-call.35 = f32[4,128,128]{1,2,0:T(8,128)S(1)} custom-call(f32[4,128,128]{2,1,0:T(8,128)S(1)} %get-tuple-element.9), custom_call_target="InvertDiagBlocksLowerTriangular" | custom-call | tf_op jit(solution)/shard_map/triangular_solve | solution.py:11
  347.6 1.0 convolution_subtract_fusion.2
  349.0 1.5 convolution_subtract_fusion.5
  354.4 3.3 fusion.17
  (78 shorter events, 14.3 us)
Async XLA Ops:
  7.2 11.2 %copy-start = (f32[2048,16]{0,1:T(8,128)S(1)}, f32[2048,16]{0,1:T(8,128)}, u32[]{:S(2)}) copy-start(f32[2048,16]{0,1:T(8,128)} %param.5) | copy-start | bytes 393220
  7.2 6.6 %copy-start.6 = (f32[4096,16]{0,1:T(8,128)S(1)}, f32[4096,16]{0,1:T(8,128)}, u32[]{:S(2)}) copy-start(f32[4096,16]{0,1:T(8,128)} %param.6) | copy-start | bytes 786436
  7.2 54.7 %all-to-all-start = ((bf16[4,2048,128]{2,1,0:T(8,128)(2,1)}), bf16[4,2048,128]{2,1,0:T(8,128)(2,1)S(1)}, u32[]{:S(2)}, u32[]{:S(2)}) async-start(bf16[4,2048,128]{2,1,0:T(8,128)(2,1)} %bitcast.66), calls=%async_computation | async-start | bytes 4194304 | tf_op jit(solution)/shard_map/all_to_all | solution.py:36
  13.7 2.0 copy-start.7
  13.7 4.6 %copy-start.8 = (f32[512]{0:T(512)S(1)}, f32[512]{0:T(512)}, u32[]{:S(2)}) copy-start(f32[512]{0:T(512)} %param.8) | copy-start | bytes 6148
  13.7 189.7 %all-reduce.4.cloned.1.call-start = ((), (), s32[]{:S(2)}) async-start(), calls=%async_computation.1 | async-start | bytes 4194304 | tf_op jit(solution)/shard_map/psum | solution.py:38
  36.2 1.3 copy-start.3
  206.2 1.7 copy-start.2
  208.1 1.0 copy-start.5
  352.8 1.6 copy-start.4
  354.4 3.3 copy-start.1
Sparse Core Ops, SparseCore 0:
  69.6 133.7 all-reduce.3
where the time goes:
time: 369 us; the launch traced here: 365 us
  waiting for transfers between devices  156 us (42%)
  other arithmetic  122 us (33%)
  matrix products  41.5 us (11%)
  local copies, waits for them, and re-layouts  21.6 us (6%)
  between operations  17.2 us (5%)
  starting transfers between devices  6.53 us (2%)
    psum x1, waiting for transfers between devices, body(): cross = lax.psum(cross_part, ('rows', 'rhs')) / count  134 us
    another operation x15, other arithmetic, body(): factor = jnp.linalg.cholesky(gram)  79.4 us
    another operation x4, other arithmetic, solve_with(): lax.linalg.triangular_solve(factor, lower, left_side=True, lower=True, tr...  39.5 us
    all_to_all x1, waiting for transfers between devices, body(): lax.all_to_all(treatment_features, 'rhs', split_axis=0, concat_axis=1, ti...  22 us
    dot_general x1, matrix products, features_of(): jnp.dot(values, freqs.T, precision=lax.Precision.HIGHEST, preferred_eleme...  17.9 us
    another operation x20, local copies, waits for them, and re-layouts  8.79 us
  transfers between devices with their start and end apart: 2, of which 2 were waited for; matrix products, arithmetic and copies ran while one was open for 7% of the time, Pallas kernels for 0%

commit v1 on v0

--- a/solution.py
+++ b/solution.py
@@ -35,7 +35,7 @@
     factor = jnp.linalg.cholesky(gram)
     targets = lax.all_to_all(treatment_features, "rhs", split_axis=0, concat_axis=1, tiled=True)
     cross_part = lax.dot_general(instruments, targets, contract, preferred_element_type=jnp.float32)
-    cross = lax.psum(cross_part, ("rows", "rhs")) / count
+    cross = jnp.sum(lax.all_gather(cross_part, ("rows", "rhs")), axis=0) / count
     coefficients = solve_with(factor, cross)
     fitted = jnp.dot(
         instruments, coefficients.astype(jnp.bfloat16), preferred_element_type=jnp.float32

time: 369 us -> 410 us (1.11)
  waiting for transfers between devices: 156 us -> 188 us
  other arithmetic: 122 us -> 133 us
    all_gather x0 -> x1, waiting for transfers between devices: none -> 59.4 us  [body(): cross = jnp.sum(lax.all_gather(cross_part, ('rows', 'rhs')), axis=0) / count]
    psum x1, waiting for transfers between devices: 134 us -> 104 us  [body(): gram = lax.psum(gram_part, ('rows', 'rhs')) / count]
    reduce_sum x0 -> x1, other arithmetic: none -> 12.3 us  [body(): cross = jnp.sum(lax.all_gather(cross_part, ('rows', 'rhs')), axis=0) / count]
    another operation x15 -> x14, other arithmetic: 79.4 us -> 78.9 us  [body(): factor = jnp.linalg.cholesky(gram)]
  transfers between devices with their start and end apart: 2 -> 3, of which waited for: 2 -> 3; matrix products, arithmetic and copies ran while one was open for 7% -> 41% of each run, Pallas kernels for 0% -> 0%
where the time goes in v1:
time: 410 us; the launch traced here: 405 us
  waiting for transfers between devices  188 us (46%)
  other arithmetic  133 us (32%)
  matrix products  38 us (9%)
  local copies, waits for them, and re-layouts  21.8 us (5%)
  between operations  17.4 us (4%)
  starting transfers between devices  6.57 us (2%)
    psum x1, waiting for transfers between devices, body(): gram = lax.psum(gram_part, ('rows', 'rhs')) / count  104 us
    another operation x14, other arithmetic, body(): factor = jnp.linalg.cholesky(gram)  78.9 us
    all_gather x1, waiting for transfers between devices, body(): cross = jnp.sum(lax.all_gather(cross_part, ('rows', 'rhs')), axis=0) / count  59.4 us
    another operation x4, other arithmetic, solve_with(): lax.linalg.triangular_solve(factor, lower, left_side=True, lower=True, tr...  40.4 us
    all_to_all x1, waiting for transfers between devices, body(): lax.all_to_all(treatment_features, 'rhs', split_axis=0, concat_axis=1, ti...  25.2 us
    dot_general x1, matrix products, features_of(): jnp.dot(values, freqs.T, precision=lax.Precision.HIGHEST, preferred_eleme...  17.9 us
    reduce_sum x1, other arithmetic, body(): cross = jnp.sum(lax.all_gather(cross_part, ('rows', 'rhs')), axis=0) / count  12.3 us
    another operation x20, local copies, waits for them, and re-layouts  11 us
  transfers between devices with their start and end apart: 3, of which 3 were waited for; matrix products, arithmetic and copies ran while one was open for 41% of the time, Pallas kernels for 0%

profile of v1, /device:TPU:0, one launch (start us, length us, event | category | flops | bytes accessed | tf_op | source)
XLA Modules:
  0.0 405.5 jit_solution(6480976726554690387)
XLA Ops:
  7.2 6.5 %all-to-all-start = ((bf16[4,2048,128]{2,1,0:T(8,128)(2,1)}), bf16[4,2048,128]{2,1,0:T(8,128)(2,1)S(1)}, u32[]{:S(2)}, u32[]{:S(2)}) async-start(bf16[4,2048,128]{2,1,0:T(8,128)(2,1)} %bitcast.68), calls=%async_computation | async-start | bytes 4194304 | tf_op jit(solution)/shard_map/all_to_all | solution.py:36
  13.7 1.9 copy.44
  15.7 2.6 gather_fusion
  18.3 17.9 %multiply_convert_fusion = bf16[512,2048]{1,0:T(8,128)(2,1)S(1)} fusion(f32[512,16]{1,0:T(8,128)S(1)} %gather_fusion, f32[2048,16]{0,1:T(8,128)S(1)} %copy-done, f32[512]{0:T(512)S(1)} %copy-done.8), kind=kOutput, calls=%fused_computation.3 | convolution fusion | flops 204472320 | bytes 2263040 | tf_op jit(solution)/shard_map/dot_general | solution.py:16
  36.3 1.3 copy-done.4
  37.6 2.3 fusion.50
  39.9 25.2 %all-to-all-done = bf16[4,2048,128]{2,1,0:T(8,128)(2,1)S(1)} async-done(((bf16[4,2048,128]{2,1,0:T(8,128)(2,1)}), bf16[4,2048,128]{2,1,0:T(8,128)(2,1)S(1)}, u32[]{:S(2)}, u32[]{:S(2)}) %all-to-all-start) | async-done | bytes 2097184 | tf_op jit(solution)/shard_map/all_to_all | solution.py:36
  65.1 3.1 copy.55
  68.3 4.5 %fusion.51 = f32[512,512]{1,0:T(8,128)} fusion(bf16[512,2048]{1,0:T(8,128)(2,1)} %copy-done.4, bf16[2048,512]{0,1:T(8,128)(2,1)} %bitcast.69), kind=kOutput, calls=%fused_computation.97 | convolution fusion | flops 1073741824 | bytes 5242880 | tf_op jit(solution)/shard_map/dot_general | solution.py:37
  72.8 103.8 %all-reduce.3.cloned.1.call-done = f32[512,512]{0,1:T(8,128)} async-done(((f32[512,512]{0,1:T(8,128)}), f32[512,512]{0,1:T(8,128)}) %all-reduce.3.cloned.1.call-update) | async-done | bytes 1048592 | tf_op jit(solution)/shard_map/psum | solution.py:33
  176.6 1.4 select_add_fusion
  178.7 11.7 %cholesky.103 = f32[128,128]{1,0:T(8,128)S(1)} custom-call(f32[128,128]{1,0:T(8,128)S(1)} %cholesky.263), custom_call_target="Cholesky" | custom-call | tf_op jit(solution)/shard_map/jit(cholesky)/cholesky | solution.py:35
  190.5 9.8 %custom-call.32 = f32[1,128,128]{1,2,0:T(8,128)S(1)} custom-call(f32[1,128,128]{2,1,0:T(8,128)S(1)} %get-tuple-element.41), custom_call_target="InvertDiagBlocksLowerTriangular" | custom-call | tf_op jit(solution)/shard_map/jit(cholesky)/cholesky | solution.py:35
  201.1 11.9 %cholesky.215 = f32[128,128]{1,0:T(8,128)S(1)} custom-call(f32[128,128]{1,0:T(8,128)S(1)} %cholesky.267), custom_call_target="Cholesky" | custom-call | tf_op jit(solution)/shard_map/jit(cholesky)/cholesky | solution.py:35
  213.1 9.8 %custom-call.33 = f32[1,128,128]{1,2,0:T(8,128)S(1)} custom-call(f32[1,128,128]{2,1,0:T(8,128)S(1)} %get-tuple-element.39), custom_call_target="InvertDiagBlocksLowerTriangular" | custom-call | tf_op jit(solution)/shard_map/jit(cholesky)/cholesky | solution.py:35
  224.0 11.7 %cholesky.236 = f32[128,128]{1,0:T(8,128)S(1)} custom-call(f32[128,128]{1,0:T(8,128)S(1)} %cholesky.272), custom_call_target="Cholesky" | custom-call | tf_op jit(solution)/shard_map/jit(cholesky)/cholesky | solution.py:35
  235.9 9.8 %custom-call.34 = f32[1,128,128]{1,2,0:T(8,128)S(1)} custom-call(f32[1,128,128]{2,1,0:T(8,128)S(1)} %get-tuple-element.37), custom_call_target="InvertDiagBlocksLowerTriangular" | custom-call | tf_op jit(solution)/shard_map/jit(cholesky)/cholesky | solution.py:35
  246.5 11.9 %cholesky.253 = f32[128,128]{1,0:T(8,128)S(1)} custom-call(f32[128,128]{1,0:T(8,128)S(1)} %convolution_subtract_fusion.8), custom_call_target="Cholesky" | custom-call | tf_op jit(solution)/shard_map/jit(cholesky)/cholesky | solution.py:35
  258.5 0.7 compare_reduce_fusion.2
  260.5 0.7 compare_reduce_fusion.1
  261.9 0.7 compare_reduce_fusion
  263.5 11.0 %while.1 = (s32[]{:T(128)}, f32[512,512]{0,1:T(8,128)S(1)}, s32[4,2]{0,1:T(2,128)S(1)}, f32[4,128,128]{2,1,0:T(8,128)}, s32[]{:T(128)}) while((s32[]{:T(128)}, f32[512,512]{0,1:T(8,128)S(1)}, s32[4,2]{0,1:T(2,128)S(1)}, f32[4,128,128]{2,1,0:T(8,128)}, s32[]{:T(128)}) %tuple.31), condition=%wide.while_cond, body=%wide.while_body.sunk | while | flops 2 | bytes 393329 | solution.py:11
  264.1 1.4 dynamic-slice.7
  266.9 1.4 dynamic-slice.7
  269.6 1.4 dynamic-slice.7
  272.4 1.4 dynamic-slice.7
  274.5 40.2 %custom-call.35 = f32[4,128,128]{1,2,0:T(8,128)S(1)} custom-call(f32[4,128,128]{2,1,0:T(8,128)} %get-tuple-element.9), custom_call_target="InvertDiagBlocksLowerTriangular" | custom-call | tf_op jit(solution)/shard_map/triangular_solve | solution.py:11
  314.7 59.4 %all-gather.3.cloned.1.call-done = f32[16384,512]{1,0:T(8,128)} async-done(((f32[512,512]{1,0:T(8,128)}), f32[16384,512]{1,0:T(8,128)}) %all-gather.3.cloned.1.call-update) | async-done | bytes 33554448 | tf_op jit(solution)/shard_map/all_gather | solution.py:38
  374.1 12.3 %reduce_sum.9 = f32[512,512]{1,0:T(8,128)S(1)} reduce(f32[32,512,512]{2,1,0:T(8,128)} %bitcast.66, f32[]{:T(128)} %constant.155.clone.1), dimensions={0}, to_apply=%region_9.10 | reduce | flops 8126464 | bytes 34603012 | tf_op jit(solution)/shard_map/reduce_sum | solution.py:38
  388.3 1.0 convolution_subtract_fusion.2
  389.7 1.5 convolution_subtract_fusion.5
  395.1 3.3 fusion.17
  (83 shorter events, 15.7 us)
Async XLA Ops:
  7.2 11.2 %copy-start = (f32[2048,16]{0,1:T(8,128)S(1)}, f32[2048,16]{0,1:T(8,128)}, u32[]{:S(2)}) copy-start(f32[2048,16]{0,1:T(8,128)} %param.5) | copy-start | bytes 393220
  7.2 6.6 %copy-start.6 = (f32[4096,16]{0,1:T(8,128)S(1)}, f32[4096,16]{0,1:T(8,128)}, u32[]{:S(2)}) copy-start(f32[4096,16]{0,1:T(8,128)} %param.6) | copy-start | bytes 786436
  7.2 57.9 %all-to-all-start = ((bf16[4,2048,128]{2,1,0:T(8,128)(2,1)}), bf16[4,2048,128]{2,1,0:T(8,128)(2,1)S(1)}, u32[]{:S(2)}, u32[]{:S(2)}) async-start(bf16[4,2048,128]{2,1,0:T(8,128)(2,1)} %bitcast.68), calls=%async_computation | async-start | bytes 4194304 | tf_op jit(solution)/shard_map/all_to_all | solution.py:36
  13.7 2.0 copy-start.7
  13.7 4.6 %copy-start.8 = (f32[512]{0:T(512)S(1)}, f32[512]{0:T(512)}, u32[]{:S(2)}) copy-start(f32[512]{0:T(512)} %param.8) | copy-start | bytes 6148
  13.7 162.9 %all-reduce.3.cloned.1.call-start = ((), (), s32[]{:S(2)}) async-start(), calls=%async_computation.1 | async-start | bytes 2097152 | tf_op jit(solution)/shard_map/psum | solution.py:33
  36.2 1.3 copy-start.4
  39.9 334.2 %all-gather.3.cloned.1.call-start = ((), (), s32[]{:S(2)}) async-start(), calls=%async_computation.2 | async-start | bytes 34603008 | tf_op jit(solution)/shard_map/all_gather | solution.py:38
  176.6 1.8 copy-start.2
  393.5 1.6 copy-start.5
  395.1 3.3 copy-start.3
  395.1 3.3 copy-start.1
Sparse Core Ops, SparseCore 0:
  40.0 136.5 all-reduce.2
  180.1 193.9 all-gather.2
